TPU v7x, 512 devices: a whole 4x8x8 slice. The times are simulated.
512 devices in a mesh: pt: 64 (over x, z, core), dir: 8 (over y).
Axes of the slice: x: 4, y: 8, z: 8, core: 2. Of those that a mesh axis runs over, the one named last changes fastest.
Arguments:
- axial: float32 [65536], P('pt'), may hold values from 0.1 to 0.3
- thrust_weight: float32 [8, 16, 65536], P('dir', None, 'pt'), may hold values from 0.5 to 2
- xdown: float32 [8, 65536], P('dir', 'pt'), may hold values from 0 to 40
- ycross: float32 [8, 65536], P('dir', 'pt'), may hold values from 0 to 4
- freq: float32 [8, 16], P('dir'), may hold values from 0.005 to 0.05
- upstream: int32 [8, 512, 16], P('dir', 'pt'), may hold values from 0 to 511, as said below
- counts: int32 [8, 512], P('dir', 'pt'), may hold values from 1 to 16
Outputs:
- power: float32 [8, 16, 65536], P('dir', None, 'pt')
- grad_axial: float32 [65536], P('pt')
Inputs may be any that keep to these rules, and one draw needn't show every extreme that they name: `upstream`: for each direction and target block the entries name distinct blocks, each owned by an index of pt at most 3 from the target block's owner; only the first counts entries are used. In each direction some target block uses blocks exactly 3 owners away on both sides.
All inputs are finite; a program needn't handle non-finite values.
Results may differ from a plain program's by a relative error of at most 0.0004.
Values sent between devices are 32-bit elements; how exact they have to be, the bound alone decides.
No kernel may reach another device: no remote copies, remote signals or barrier semaphores. Data moves between devices by JAX's collectives and lax.ppermute only.
A program may use at most 64 MiB of HBM per device.

v0:
```python
import jax
import jax.numpy as jnp
from jax import lax
from jax.sharding import PartitionSpec as P

BLOCK = 128
GRID = 5
SPEEDS = 16
REACH = 3


SIGMA_ZERO = 0.5
EXPANSION = 0.03
STRENGTH_SCALE = 0.25
ROTOR_SPAN = 0.8


def from_behind(value, axis, by):
    length = lax.axis_size(axis)
    pairs = [(i, i + by) for i in range(length) if 0 <= i + by < length]
    return lax.ppermute(value, axis, pairs)


def rotor_points():
    points = jnp.arange(GRID * GRID, dtype=jnp.int32)
    across = ROTOR_SPAN * ((points % GRID).astype(jnp.float32) / (GRID - 1) - 0.5)
    upward = ROTOR_SPAN * ((points // GRID).astype(jnp.float32) / (GRID - 1) - 0.5)
    return (across, upward)


def wind_speeds():
    return 0.4 + 0.75 * jnp.arange(SPEEDS, dtype=jnp.float32) / (SPEEDS - 1)


def kernel_tile(target_x, target_y, source_x, source_y):
    across, upward = rotor_points()
    ahead_dist = jnp.maximum(target_x[None, None, :] - source_x[:, None, None], 0.0)
    spread_width = SIGMA_ZERO + EXPANSION * ahead_dist
    lateral = target_y[None, None, :] + across[None, :, None] - source_y[:, None, None]
    spread = lateral * lateral + (upward * upward)[None, :, None]
    width_ratio = SIGMA_ZERO / spread_width
    kernel = (
        STRENGTH_SCALE
        * width_ratio
        * width_ratio
        * (1.0 - jnp.exp(-ahead_dist))
        * jnp.exp(-spread / (2.0 * spread_width * spread_width))
    )
    return kernel.reshape(source_x.shape[0], -1).astype(jnp.bfloat16)


def body(axial, thrust_weight, xdown, ycross, freq, upstream, counts):
    speeds = wind_speeds()
    rotor_count = GRID * GRID
    local_turbines = axial.shape[0]
    local_blocks = local_turbines // BLOCK
    slot_total = upstream.shape[2]
    position = lax.axis_index("pt")
    lowest = (position - REACH) * local_blocks
    power_coef = 4.0 * axial * (1.0 - axial) ** 2
    slope_coef = 4.0 * (1.0 - axial) * (1.0 - 3.0 * axial)
    weights = freq[0]
    strength = axial[None, :] * thrust_weight[0]
    packed = jnp.concatenate([strength, xdown[0][None, :], ycross[0][None, :]], axis=0)
    pieces = [packed for offset in range(2 * REACH + 1)]
    for offset in range(2 * REACH + 1):
        if offset != REACH:
            pieces[offset] = from_behind(packed, "pt", REACH - offset)
    source_rows = jnp.concatenate(pieces, axis=1)
    source_strength = source_rows[:SPEEDS].astype(jnp.bfloat16)
    source_x = source_rows[SPEEDS]
    source_y = source_rows[SPEEDS + 1]
    back_width = (2 * REACH + 1) * local_turbines
    local_x = xdown[0]
    local_y = ycross[0]

    def one_block(block_index, state_pair):
        cube_means, back_sum = state_pair
        first_turbine = (block_index * BLOCK).astype(jnp.int32)
        target_x = lax.dynamic_slice_in_dim(local_x, first_turbine, BLOCK)
        target_y = lax.dynamic_slice_in_dim(local_y, first_turbine, BLOCK)
        listed = upstream[0, block_index]
        in_use = counts[0, block_index]

        def forward(slot_index, carried):
            deficit, kernel_stack = carried
            column = (listed[slot_index] - lowest) * BLOCK
            kernel = kernel_tile(
                target_x,
                target_y,
                lax.dynamic_slice_in_dim(source_x, column, BLOCK),
                lax.dynamic_slice_in_dim(source_y, column, BLOCK),
            )
            source_block = lax.dynamic_slice_in_dim(source_strength, column, BLOCK, 1)
            deficit = deficit + jnp.dot(source_block, kernel, preferred_element_type=jnp.float32)
            kernel_stack = lax.dynamic_update_index_in_dim(kernel_stack, kernel, slot_index, 0)
            return (deficit, kernel_stack)

        start_forward = (
            jnp.zeros((SPEEDS, rotor_count * BLOCK), jnp.float32),
            jnp.zeros((slot_total, BLOCK, rotor_count * BLOCK), jnp.bfloat16),
        )
        deficit, kernel_stack = lax.fori_loop(0, in_use, forward, start_forward)
        velocity = (speeds[:, None] / (1.0 + deficit)).reshape(SPEEDS, rotor_count, BLOCK)
        cube_mean = jnp.mean(velocity**3, axis=1)
        power_block = lax.dynamic_slice_in_dim(power_coef, first_turbine, BLOCK)
        factor = weights[:, None, None] * power_block[None, None, :] * (3.0 / rotor_count)
        adjoint = -factor * velocity**4 / speeds[:, None, None]
        adjoint = adjoint.reshape(SPEEDS, rotor_count * BLOCK).astype(jnp.bfloat16)

        def backward(slot_index, back_sum):
            kernel = lax.dynamic_index_in_dim(kernel_stack, slot_index, 0, keepdims=False)
            target_column = (listed[slot_index] - lowest) * BLOCK
            back_term = lax.dot_general(
                adjoint, kernel, (((1,), (1,)), ((), ())), preferred_element_type=jnp.float32
            )
            current = lax.dynamic_slice_in_dim(back_sum, target_column, BLOCK, 1)
            return lax.dynamic_update_slice_in_dim(back_sum, current + back_term, target_column, 1)

        back_sum = lax.fori_loop(0, in_use, backward, back_sum)
        cube_means = lax.dynamic_update_slice_in_dim(cube_means, cube_mean, first_turbine, 1)
        return (cube_means, back_sum)

    start_state = (
        jnp.zeros((SPEEDS, local_turbines), jnp.float32),
        jnp.zeros((SPEEDS, back_width), jnp.float32),
    )
    cube_means, back_sum = lax.fori_loop(0, local_blocks, one_block, start_state)
    returned = back_sum[:, REACH * local_turbines : (REACH + 1) * local_turbines]
    for offset in range(2 * REACH + 1):
        if offset != REACH:
            slice_part = back_sum[:, offset * local_turbines : (offset + 1) * local_turbines]
            returned = returned + from_behind(slice_part, "pt", offset - REACH)
    powers = [power_coef[None, :] * cube_means]
    gradient = jnp.sum(
        weights[:, None] * (slope_coef[None, :] * cube_means + thrust_weight[0] * returned), axis=0
    )
    gradient = lax.psum(gradient, "dir")
    return (jnp.stack(powers), gradient)


def solution(mesh):
    placed = (
        P("pt"),
        P("dir", None, "pt"),
        P("dir", "pt"),
        P("dir", "pt"),
        P("dir", None),
        P("dir", "pt", None),
        P("dir", "pt"),
    )
    return jax.shard_map(
        body, mesh=mesh, in_specs=placed, out_specs=(P("dir", None, "pt"), P("pt")), check_vma=False
    )
```

profile of v0, /device:TPU:6, one launch (start us, length us, event | category | flops | bytes accessed | tf_op | source)
XLA Modules:
  0.0 1129.3 jit_solution(14063898668800314735)
XLA Ops:
  31.5 309.4 %while.97 = (s32[]{:T(128)}, f32[16,1024]{1,0:T(8,128)S(1)}, f32[16,7168]{1,0:T(8,128)S(1)}, s32[1,8]{1,0:T(1,128)S(1)}, s32[1,8,16]{2,1,0:T(8,128)}, /*index=5*...) while((s32[]{:T(128)}, f32[16,1024]{1,0:T(8,128)S(1)}, ...), condition=%wide.region_6.7_spmd.clone.clone, body=%wide.region_0.6_spmd.clone.clone.sunk | while | flops 32720584 | bytes 19203840 | solution.py:128
  34.4 7.2 broadcast.546
  41.6 11.8 %while.98 = (s32[]{:T(128)}, f32[16,3200]{1,0:T(8,128)S(1)}, bf16[16,128,3200]{1,2,0:T(8,128)(2,1)}, s32[]{:T(128)}, s32[16]{0:T(128)S(1)}, /*index=5*/s32[]{:T(...) while((s32[]{:T(128)}, f32[16,3200]{1,0:T(8,128)S(1)}, ...), condition=%wide.region_2.2_spmd, body=%wide.region_1.1_spmd.sunk | while | flops 19093144 | bytes 3372189 | solution.py:103
  53.8 7.4 while.99
  64.1 7.2 broadcast.546
  71.4 22.9 %while.98 = (s32[]{:T(128)}, f32[16,3200]{1,0:T(8,128)S(1)}, bf16[16,128,3200]{1,2,0:T(8,128)(2,1)}, s32[]{:T(128)}, s32[16]{0:T(128)S(1)}, /*index=5*/s32[]{:T(...) while((s32[]{:T(128)}, f32[16,3200]{1,0:T(8,128)S(1)}, ...), condition=%wide.region_2.2_spmd, body=%wide.region_1.1_spmd.sunk | while | flops 19093144 | bytes 3372189 | solution.py:103
  94.7 14.1 %while.99 = (s32[]{:T(128)}, f32[16,7168]{1,0:T(8,128)S(1)}, s32[]{:T(128)}, s32[16]{0:T(128)S(1)}, s32[]{:T(128)}, /*index=5*/bf16[16,128,3200]{1,2,0:T(8,128)(...) while((s32[]{:T(128)}, f32[16,7168]{1,0:T(8,128)S(1)}, ...), condition=%wide.region_5.5_spmd, body=%wide.region_4.4_spmd.sunk | while | flops 13109258 | bytes 938213 | solution.py:120
  111.8 7.2 broadcast.546
  119.0 22.9 %while.98 = (s32[]{:T(128)}, f32[16,3200]{1,0:T(8,128)S(1)}, bf16[16,128,3200]{1,2,0:T(8,128)(2,1)}, s32[]{:T(128)}, s32[16]{0:T(128)S(1)}, /*index=5*/s32[]{:T(...) while((s32[]{:T(128)}, f32[16,3200]{1,0:T(8,128)S(1)}, ...), condition=%wide.region_2.2_spmd, body=%wide.region_1.1_spmd.sunk | while | flops 19093144 | bytes 3372189 | solution.py:103
  142.3 14.1 %while.99 = (s32[]{:T(128)}, f32[16,7168]{1,0:T(8,128)S(1)}, s32[]{:T(128)}, s32[16]{0:T(128)S(1)}, s32[]{:T(128)}, /*index=5*/bf16[16,128,3200]{1,2,0:T(8,128)(...) while((s32[]{:T(128)}, f32[16,7168]{1,0:T(8,128)S(1)}, ...), condition=%wide.region_5.5_spmd, body=%wide.region_4.4_spmd.sunk | while | flops 13109258 | bytes 938213 | solution.py:120
  159.4 7.2 broadcast.546
  166.6 22.9 %while.98 = (s32[]{:T(128)}, f32[16,3200]{1,0:T(8,128)S(1)}, bf16[16,128,3200]{1,2,0:T(8,128)(2,1)}, s32[]{:T(128)}, s32[16]{0:T(128)S(1)}, /*index=5*/s32[]{:T(...) while((s32[]{:T(128)}, f32[16,3200]{1,0:T(8,128)S(1)}, ...), condition=%wide.region_2.2_spmd, body=%wide.region_1.1_spmd.sunk | while | flops 19093144 | bytes 3372189 | solution.py:103
  189.9 14.1 %while.99 = (s32[]{:T(128)}, f32[16,7168]{1,0:T(8,128)S(1)}, s32[]{:T(128)}, s32[16]{0:T(128)S(1)}, s32[]{:T(128)}, /*index=5*/bf16[16,128,3200]{1,2,0:T(8,128)(...) while((s32[]{:T(128)}, f32[16,7168]{1,0:T(8,128)S(1)}, ...), condition=%wide.region_5.5_spmd, body=%wide.region_4.4_spmd.sunk | while | flops 13109258 | bytes 938213 | solution.py:120
  207.0 7.2 broadcast.546
  214.2 22.9 %while.98 = (s32[]{:T(128)}, f32[16,3200]{1,0:T(8,128)S(1)}, bf16[16,128,3200]{1,2,0:T(8,128)(2,1)}, s32[]{:T(128)}, s32[16]{0:T(128)S(1)}, /*index=5*/s32[]{:T(...) while((s32[]{:T(128)}, f32[16,3200]{1,0:T(8,128)S(1)}, ...), condition=%wide.region_2.2_spmd, body=%wide.region_1.1_spmd.sunk | while | flops 19093144 | bytes 3372189 | solution.py:103
  237.5 14.1 %while.99 = (s32[]{:T(128)}, f32[16,7168]{1,0:T(8,128)S(1)}, s32[]{:T(128)}, s32[16]{0:T(128)S(1)}, s32[]{:T(128)}, /*index=5*/bf16[16,128,3200]{1,2,0:T(8,128)(...) while((s32[]{:T(128)}, f32[16,7168]{1,0:T(8,128)S(1)}, ...), condition=%wide.region_5.5_spmd, body=%wide.region_4.4_spmd.sunk | while | flops 13109258 | bytes 938213 | solution.py:120
  254.6 7.2 broadcast.546
  261.8 6.2 while.98
  275.4 7.2 broadcast.546
  282.6 22.9 %while.98 = (s32[]{:T(128)}, f32[16,3200]{1,0:T(8,128)S(1)}, bf16[16,128,3200]{1,2,0:T(8,128)(2,1)}, s32[]{:T(128)}, s32[16]{0:T(128)S(1)}, /*index=5*/s32[]{:T(...) while((s32[]{:T(128)}, f32[16,3200]{1,0:T(8,128)S(1)}, ...), condition=%wide.region_2.2_spmd, body=%wide.region_1.1_spmd.sunk | while | flops 19093144 | bytes 3372189 | solution.py:103
  305.9 14.1 %while.99 = (s32[]{:T(128)}, f32[16,7168]{1,0:T(8,128)S(1)}, s32[]{:T(128)}, s32[16]{0:T(128)S(1)}, s32[]{:T(128)}, /*index=5*/bf16[16,128,3200]{1,2,0:T(8,128)(...) while((s32[]{:T(128)}, f32[16,7168]{1,0:T(8,128)S(1)}, ...), condition=%wide.region_5.5_spmd, body=%wide.region_4.4_spmd.sunk | while | flops 13109258 | bytes 938213 | solution.py:120
  323.0 7.2 broadcast.546
  342.9 18.9 %collective-permute-start.11 = (f32[16,1024]{1,0:T(8,128)S(1)}, f32[16,1024]{1,0:T(8,128)S(1)}, u32[]{:S(2)}, u32[]{:S(2)}) collective-permute-start(f32[16,1024]{1,0:T(8,128)S(1)} %get-tuple-element.750), channel_id=1, source_target_pairs={{0,24},{8,32},{16,40},{24,48},{32,56},{40,64},{48,72},{56,80},{64,... | collective-permute-start | bytes 196616 | tf_op jit(solution)/shard_map/ppermute | solution.py:21
  379.8 749.5 %psum.7 = f32[1024]{0:T(1024)} all-reduce(f32[1024]{0:T(1024)S(1)} %get-tuple-element.752), channel_id=1, replica_groups=mesh['pt'=64,'dir'=8] {'dir'}, use_global_device_ids=true, to_apply=%region_8.9 | all-reduce | flops 1024 | bytes 8192 | tf_op jit(solution)/shard_map/psum | solution.py:138
  (464 shorter events, 240.4 us)
Async XLA Ops:
  0.6 30.9 %copy-start.1 = (f32[1,16]{1,0:T(1,128)S(1)}, f32[1,16]{1,0:T(1,128)}, u32[]{:S(2)}) copy-start(f32[1,16]{1,0:T(1,128)} %param.17) | copy-start | bytes 196
  0.6 30.9 %copy-start.2 = (s32[1,8]{1,0:T(1,128)S(1)}, s32[1,8]{1,0:T(1,128)}, u32[]{:S(2)}) copy-start(s32[1,8]{1,0:T(1,128)} %param.19) | copy-start | bytes 100
  2.2 21.4 %collective-permute-start = (f32[18,1024]{1,0:T(8,128)S(1)}, f32[18,1024]{1,0:T(8,128)S(1)}, u32[]{:S(2)}, u32[]{:S(2)}) collective-permute-start(f32[18,1024]{1,0:T(8,128)S(1)} %pad_maximum_fusion), channel_id=1, source_target_pairs={{0,24},{8,32},{16,40},{24,48},{32,56},{40,64},{48,72},{56,80},{64,... | collective-permute-start | bytes 221192 | tf_op jit(solution)/shard_map/ppermute | solution.py:21
  6.0 20.7 %collective-permute-start.1 = (f32[18,1024]{1,0:T(8,128)S(1)}, f32[18,1024]{1,0:T(8,128)S(1)}, u32[]{:S(2)}, u32[]{:S(2)}) collective-permute-start(f32[18,1024]{1,0:T(8,128)S(1)} %pad_maximum_fusion), channel_id=1, source_target_pairs={{0,16},{8,24},{16,32},{24,40},{32,48},{40,56},{48,64},{56,72},{64,... | collective-permute-start | bytes 221192 | tf_op jit(solution)/shard_map/ppermute | solution.py:21
  10.2 16.5 %collective-permute-start.2 = (f32[18,1024]{1,0:T(8,128)S(1)}, f32[18,1024]{1,0:T(8,128)S(1)}, u32[]{:S(2)}, u32[]{:S(2)}) collective-permute-start(f32[18,1024]{1,0:T(8,128)S(1)} %pad_maximum_fusion), channel_id=1, source_target_pairs={{0,8},{8,16},{16,24},{24,32},{32,40},{40,48},{48,56},{56,64},{64,7... | collective-permute-start | bytes 221192 | tf_op jit(solution)/shard_map/ppermute | solution.py:21
  14.4 13.1 %collective-permute-start.3 = (f32[18,1024]{1,0:T(8,128)S(1)}, f32[18,1024]{1,0:T(8,128)S(1)}, u32[]{:S(2)}, u32[]{:S(2)}) collective-permute-start(f32[18,1024]{1,0:T(8,128)S(1)} %pad_maximum_fusion), channel_id=1, source_target_pairs={{8,0},{16,8},{24,16},{32,24},{40,32},{48,40},{56,48},{64,56},{72,6... | collective-permute-start | bytes 221192 | tf_op jit(solution)/shard_map/ppermute | solution.py:21
  18.7 8.8 collective-permute-start.4
  23.6 7.8 collective-permute-start.5
  31.5 347.6 %copy-start = (f32[1,16,1024]{2,1,0:T(8,128)S(1)}, f32[1,16,1024]{2,1,0:T(8,128)}, u32[]{:S(2)}) copy-start(f32[1,16,1024]{2,1,0:T(8,128)} %param.14) | copy-start | bytes 196612
  341.0 30.5 %collective-permute-start.10 = (f32[16,1024]{1,0:T(8,128)S(1)}, f32[16,1024]{1,0:T(8,128)S(1)}, u32[]{:S(2)}, u32[]{:S(2)}) collective-permute-start(f32[16,1024]{1,0:T(8,128)S(1)} %get-tuple-element.751), channel_id=1, source_target_pairs={{0,16},{8,24},{16,32},{24,40},{32,48},{40,56},{48,64},{56,72},{64,... | collective-permute-start | bytes 196616 | tf_op jit(solution)/shard_map/ppermute | solution.py:21
  342.9 31.0 %collective-permute-start.11 = (f32[16,1024]{1,0:T(8,128)S(1)}, f32[16,1024]{1,0:T(8,128)S(1)}, u32[]{:S(2)}, u32[]{:S(2)}) collective-permute-start(f32[16,1024]{1,0:T(8,128)S(1)} %get-tuple-element.750), channel_id=1, source_target_pairs={{0,24},{8,32},{16,40},{24,48},{32,56},{40,64},{48,72},{56,80},{64,... | collective-permute-start | bytes 196616 | tf_op jit(solution)/shard_map/ppermute | solution.py:21
  361.8 12.1 %collective-permute-start.6 = (f32[16,1024]{1,0:T(8,128)S(1)}, f32[16,1024]{1,0:T(8,128)S(1)}, u32[]{:S(2)}, u32[]{:S(2)}) collective-permute-start(f32[16,1024]{1,0:T(8,128)S(1)} %get-tuple-element.746), channel_id=1, source_target_pairs={{24,0},{32,8},{40,16},{48,24},{56,32},{64,40},{72,48},{80,56},{88,... | collective-permute-start | bytes 196616 | tf_op jit(solution)/shard_map/ppermute | solution.py:21
  363.7 10.1 collective-permute-start.7
  369.5 4.4 collective-permute-start.8
  371.4 7.7 collective-permute-start.9
where the time goes:
time: 1140 us; the launch traced here: 1130 us
  blocking collectives  750 us (66%)
  local copies, waits for them, and re-layouts  121 us (11%)
  loops' own time  76 us (7%)
  other arithmetic  75 us (7%)
  starting transfers between devices  56.5 us (5%)
  matrix products  41.1 us (4%)
    psum x1, blocking collectives, body(): gradient = lax.psum(gradient, 'dir')  750 us
    another operation x16, local copies, waits for them, and re-layouts  57.9 us
    ppermute x12, starting transfers between devices, from_behind(): return lax.ppermute(value, axis, pairs)  56.5 us
    dynamic_update_slice x24, other arithmetic, forward(): lax.dynamic_update_index_in_dim(kernel_stack, kernel, slot_index, 0)  44 us
    another operation x8, loops' own time, one_block(): deficit, kernel_stack = lax.fori_loop(0, in_use, forward, start_forward)  38 us
    another operation x8, loops' own time, one_block(): back_sum = lax.fori_loop(0, in_use, backward, back_sum)  37.3 us
    dot_general x24, matrix products, backward(): lax.dot_general(adjoint, kernel, (((1,), (1,)), ((), ())), preferred_elem...  32.9 us
  transfers between devices with their start and end apart: 12, of which 2 were waited for; matrix products, arithmetic and copies ran while one was open for 0% of the time, Pallas kernels for 0%

commit v1 on v0

v1 whole, which is shorter than its diff:
```python
import functools
import math
import jax
import jax.numpy as jnp
from jax import lax
from jax.experimental import pallas as pl
from jax.experimental.pallas import tpu as pltpu
from jax.sharding import PartitionSpec as P

BLOCK = 128
BLKS = 8
GRID = 5
SPEEDS = 16
REACH = 3
PIECES = 2 * REACH + 1
SOURCES = PIECES * BLKS
NULL = SOURCES
PAIRS = 16
ROWS = 16
CHUNKS = BLOCK // ROWS
LANES = 16 * ROWS
LOG2E = math.log2(math.e)
Y_SCALE = math.sqrt(2.0 * LOG2E)
STEP = 0.2 * Y_SCALE
WIDEN = 0.06 / LOG2E


def from_behind(value, axis, by):
    length = lax.axis_size(axis)
    pairs = [(i, i + by) for i in range(length) if 0 <= i + by < length]
    return lax.ppermute(value, axis, pairs)


def wake_tiles(target_x, target_y, source_x, source_y):
    behind = jnp.minimum(source_x - target_x, 0.0)
    ratio = 1.0 / (1.0 - WIDEN * behind)
    q = ratio * ratio
    amp = q - q * jnp.exp2(behind)
    lateral = target_y - source_y
    lateral_q = lateral * q
    centre = amp * jnp.exp2(-(lateral * lateral_q))
    tilt = (2.0 * STEP) * lateral_q
    u1 = jnp.exp2(-(STEP * STEP) * q)
    right = jnp.exp2(-tilt) * u1
    left = jnp.exp2(tilt) * u1
    u2 = u1 * u1
    u4 = u2 * u2
    right1 = centre * right
    left1 = centre * left
    right2 = right1 * (right * u2)
    left2 = left1 * (left * u2)
    base = [left2, left1, centre, right1, right2]
    return base + [k * u1 for k in base] + [k * u4 for k in base]


def farm_kernel(index_ref, pairs_ref, *refs):
    pieces = refs[:PIECES]
    axial_ref, spread_ref, freq_ref = refs[PIECES : PIECES + 3]
    power_ref, direct_ref = refs[PIECES + 3 : PIECES + 5]
    back_refs = refs[PIECES + 5 : 2 * PIECES + 5]
    s_ref, xs_ref, ys_ref, xt_ref, yt_ref, d_ref, a_ref, k_ref, b_ref = refs[2 * PIECES + 5 :]

    for o in range(PIECES):
        for blk in range(BLKS):
            q = o * BLKS + blk
            s_ref[q] = (pieces[o][blk * SPEEDS : (blk + 1) * SPEEDS, :].astype(jnp.bfloat16).astype(jnp.float32) * 0.25).astype(jnp.bfloat16)
            row = SPEEDS * BLKS + blk
            xs_ref[q] = jnp.broadcast_to(pieces[o][row : row + 1, :] * LOG2E, (8, BLOCK))
            row = row + BLKS
            ys_ref[q] = jnp.broadcast_to(pieces[o][row : row + 1, :] * Y_SCALE, (8, BLOCK))
            b_ref[q] = jnp.zeros((SPEEDS, BLOCK), jnp.float32)
    s_ref[NULL] = jnp.zeros((SPEEDS, BLOCK), jnp.bfloat16)
    xs_ref[NULL] = jnp.full((8, BLOCK), 1e6, jnp.float32)
    ys_ref[NULL] = jnp.zeros((8, BLOCK), jnp.float32)
    b_ref[NULL] = jnp.zeros((SPEEDS, BLOCK), jnp.float32)

    freq = freq_ref[...]
    speed = 0.4 + 0.75 * lax.broadcasted_iota(jnp.int32, (SPEEDS, BLOCK), 0).astype(jnp.float32) / (SPEEDS - 1)
    lane = lax.broadcasted_iota(jnp.int32, (SPEEDS, BLOCK), 1)
    low_weight = jnp.where(lane < 5 * ROWS, 1.0, 2.0)
    high_weight = jnp.where(lane < 7 * ROWS, 2.0, 0.0)
    scale = freq * (-0.25 * 3.0 / (GRID * GRID)) / speed

    def one_block(b, carry):
        own = REACH * BLKS + b
        xt_ref[...] = jnp.transpose(jnp.broadcast_to(xs_ref[own][0:1, :], (BLOCK, BLOCK)))
        yt_ref[...] = jnp.transpose(jnp.broadcast_to(ys_ref[own][0:1, :], (BLOCK, BLOCK)))
        d_ref[...] = jnp.zeros_like(d_ref)
        count = pairs_ref[b]

        def forward(p, carry):
            q0 = index_ref[b, 2 * p]
            q1 = index_ref[b, 2 * p + 1]
            strength = jnp.concatenate([s_ref[q0], s_ref[q1]], axis=1)
            sx = [jnp.concatenate([xs_ref[q]] * 2, axis=0) for q in (q0, q1)]
            sy = [jnp.concatenate([ys_ref[q]] * 2, axis=0) for q in (q0, q1)]
            zero = jnp.zeros((ROWS, 2 * BLOCK), jnp.bfloat16)
            for tc in range(CHUNKS):
                tx = xt_ref[tc * ROWS : (tc + 1) * ROWS, :]
                ty = yt_ref[tc * ROWS : (tc + 1) * ROWS, :]
                halves = [wake_tiles(tx, ty, sx[h], sy[h]) for h in range(2)]
                kernel = jnp.concatenate(
                    [jnp.concatenate([k0.astype(jnp.bfloat16), k1.astype(jnp.bfloat16)], axis=1) for k0, k1 in zip(*halves)] + [zero],
                    axis=0,
                )
                k_ref[p, tc * LANES : (tc + 1) * LANES, :] = kernel
                d_ref[tc] += lax.dot_general(strength, kernel, (((1,), (1,)), ((), ())), preferred_element_type=jnp.float32)
            return carry

        lax.fori_loop(0, count, forward, 0)

        cube = jnp.zeros((SPEEDS, BLOCK), jnp.float32)
        for tc in range(CHUNKS):
            coef = spread_ref[b, tc : tc + 1, :] * scale
            v_low = speed / (1.0 + d_ref[tc, :, :BLOCK])
            v_high = speed / (1.0 + d_ref[tc, :, BLOCK:])
            s_low = v_low * v_low
            s_high = v_high * v_high
            a_ref[:, tc * LANES : tc * LANES + BLOCK] = (coef * low_weight * (s_low * s_low)).astype(jnp.bfloat16)
            a_ref[:, tc * LANES + BLOCK : (tc + 1) * LANES] = (coef * high_weight * (s_high * s_high)).astype(jnp.bfloat16)
            total = low_weight * (s_low * v_low) + high_weight * (s_high * v_high)
            total = total + pltpu.roll(total, 64, 1)
            total = total + pltpu.roll(total, 32, 1)
            total = total + pltpu.roll(total, 16, 1)
            cube = jnp.where(lane // ROWS == tc, total, cube)
        cube = cube * (1.0 / (GRID * GRID))
        axial = axial_ref[pl.ds(b, 1), :]
        power_coef = 4.0 * axial * (1.0 - axial) * (1.0 - axial)
        slope_coef = 4.0 * (1.0 - axial) * (1.0 - 3.0 * axial)
        power_ref[:, pl.ds(pl.multiple_of(b * BLOCK, BLOCK), BLOCK)] = power_coef * cube
        direct_ref[pl.ds(b, 1), :] = jnp.sum(freq * (slope_coef * cube), axis=0, keepdims=True)

        def backward(p, carry):
            term = jnp.dot(a_ref[...], k_ref[p], preferred_element_type=jnp.float32)
            b_ref[index_ref[b, 2 * p]] += term[:, :BLOCK]
            b_ref[index_ref[b, 2 * p + 1]] += term[:, BLOCK:]
            return carry

        lax.fori_loop(0, count, backward, 0)
        return carry

    lax.fori_loop(0, BLKS, one_block, 0)
    for o in range(PIECES):
        rows = []
        for blk in range(BLKS):
            strength = pieces[o][blk * SPEEDS : (blk + 1) * SPEEDS, :]
            rows.append(jnp.sum(freq * strength * b_ref[o * BLKS + blk], axis=0, keepdims=True))
        back_refs[o][...] = jnp.concatenate(rows, axis=0)


def farm(index, pairs, pieces, axial, spread, freq):
    f32 = jnp.float32
    smem = pl.BlockSpec(memory_space=pltpu.SMEM)
    vmem = pl.BlockSpec(memory_space=pltpu.VMEM)
    piece = jax.ShapeDtypeStruct((BLKS, BLOCK), f32)
    return pl.pallas_call(
        farm_kernel,
        name="farm",
        out_shape=(jax.ShapeDtypeStruct((SPEEDS, BLKS * BLOCK), f32), piece) + (piece,) * PIECES,
        in_specs=[smem, smem] + [vmem] * (PIECES + 3),
        out_specs=(vmem,) * (PIECES + 2),
        scratch_shapes=[
            pltpu.VMEM((SOURCES + 1, SPEEDS, BLOCK), jnp.bfloat16),
            pltpu.VMEM((SOURCES + 1, 8, BLOCK), f32),
            pltpu.VMEM((SOURCES + 1, 8, BLOCK), f32),
            pltpu.VMEM((BLOCK, BLOCK), f32),
            pltpu.VMEM((BLOCK, BLOCK), f32),
            pltpu.VMEM((CHUNKS, SPEEDS, LANES), f32),
            pltpu.VMEM((SPEEDS, CHUNKS * LANES), jnp.bfloat16),
            pltpu.VMEM((PAIRS // 2, CHUNKS * LANES, 2 * BLOCK), jnp.bfloat16),
            pltpu.VMEM((SOURCES + 1, SPEEDS, BLOCK), f32),
        ],
        compiler_params=pltpu.CompilerParams(vmem_limit_bytes=32 << 20),
        cost_estimate=pl.CostEstimate(flops=2 * 64 * 128 * 2048 * 16 * 2, bytes_accessed=4 << 20, transcendentals=0),
    )(index, pairs, *pieces, axial, spread, freq)


def body(axial, thrust_weight, xdown, ycross, freq, upstream, counts):
    position = lax.axis_index("pt")
    lowest = (position - REACH) * BLKS
    strength = (axial[None, :] * thrust_weight[0]).reshape(SPEEDS, BLKS, BLOCK)
    strength = jnp.transpose(strength, (1, 0, 2)).reshape(BLKS * SPEEDS, BLOCK)
    packed = jnp.concatenate([strength, xdown[0].reshape(BLKS, BLOCK), ycross[0].reshape(BLKS, BLOCK)], axis=0)
    pieces = [packed if o == REACH else from_behind(packed, "pt", REACH - o) for o in range(PIECES)]
    slots = lax.broadcasted_iota(jnp.int32, (BLKS, PAIRS), 1)
    index = jnp.where(slots < counts[0][:, None], upstream[0] - lowest, NULL)
    pairs = (counts[0] + 1) // 2
    axial_rows = axial.reshape(BLKS, BLOCK)
    power_coef = 4.0 * axial_rows * (1.0 - axial_rows) ** 2
    spread = jnp.broadcast_to(power_coef.reshape(BLKS, CHUNKS, 1, ROWS), (BLKS, CHUNKS, BLOCK // ROWS, ROWS)).reshape(BLKS, CHUNKS, BLOCK)
    freq_wide = jnp.broadcast_to(freq[0][:, None], (SPEEDS, BLOCK))
    power, direct, *back = farm(index, pairs, pieces, axial_rows, spread, freq_wide)
    total = back[REACH]
    for o in range(PIECES):
        if o != REACH:
            total = total + from_behind(back[o], "pt", o - REACH)
    gradient = direct + total / axial_rows
    for bit in (1, 2, 4):
        gradient = gradient + lax.ppermute(gradient, "dir", [(i, i ^ bit) for i in range(lax.axis_size("dir"))])
    return power[None], gradient.reshape(-1)


def solution(mesh):
    placed = (
        P("pt"),
        P("dir", None, "pt"),
        P("dir", "pt"),
        P("dir", "pt"),
        P("dir", None),
        P("dir", "pt", None),
        P("dir", "pt"),
    )
    return jax.shard_map(
        body, mesh=mesh, in_specs=placed, out_specs=(P("dir", None, "pt"), P("pt")), check_vma=False
    )
```

time: 1140 us -> 115 us (0.10)
  the two profiles are of different devices: /device:TPU:6 before, /device:TPU:18 now
where the time goes in v1:
time: 115 us; the launch traced here: 114 us
  starting transfers between devices  55.9 us (49%)
  Pallas kernels  30 us (26%)
  waiting for transfers between devices  24.1 us (21%)
  local copies, waits for them, and re-layouts  2.52 us (2%)
    ppermute x12, starting transfers between devices, from_behind(): return lax.ppermute(value, axis, pairs)  50.2 us
    pallas_call x1, Pallas kernels, farm(): pl.pallas_call(farm_kernel, name='farm', out_shape=(jax.ShapeDtypeStruct(...  30 us
    ppermute x3, waiting for transfers between devices, body(): lax.ppermute(gradient, 'dir', [(i, i ^ bit) for i in range(lax.axis_size(...  15.5 us
    ppermute x12, waiting for transfers between devices, from_behind(): return lax.ppermute(value, axis, pairs)  8.56 us
    ppermute x3, starting transfers between devices, body(): lax.ppermute(gradient, 'dir', [(i, i ^ bit) for i in range(lax.axis_size(...  5.74 us
  transfers between devices with their start and end apart: 15, of which 5 were waited for; matrix products, arithmetic and copies ran while one was open for 0% of the time, Pallas kernels for 0%

profile of v1, /device:TPU:18, one launch (start us, length us, event | category | flops | bytes accessed | tf_op | source)
XLA Modules:
  0.0 114.1 jit_solution(814690095037671532)
XLA Ops:
  0.6 0.9 copy.10
  1.6 0.6 copy-done.2
  2.2 3.7 %collective-permute-start = (f32[144,128]{1,0:T(8,128)S(1)}, f32[144,128]{1,0:T(8,128)S(1)}, u32[]{:S(2)}, u32[]{:S(2)}) collective-permute-start(f32[144,128]{1,0:T(8,128)S(1)} %pad_maximum_fusion.refs_3_), channel_id=1, source_target_pairs={{0,24},{8,32},{16,40},{24,48},{32,56},{40,64},{48,72},{56,80},{64,... | collective-permute-start | bytes 221192 | tf_op jit(solution)/shard_map/ppermute | solution.py:31
  6.0 4.3 %collective-permute-start.1 = (f32[144,128]{1,0:T(8,128)S(1)}, f32[144,128]{1,0:T(8,128)S(1)}, u32[]{:S(2)}, u32[]{:S(2)}) collective-permute-start(f32[144,128]{1,0:T(8,128)S(1)} %pad_maximum_fusion.refs_3_), channel_id=1, source_target_pairs={{0,16},{8,24},{16,32},{24,40},{32,48},{40,56},{48,64},{56,72},{64,... | collective-permute-start | bytes 221192 | tf_op jit(solution)/shard_map/ppermute | solution.py:31
  10.2 4.1 %collective-permute-start.2 = (f32[144,128]{1,0:T(8,128)S(1)}, f32[144,128]{1,0:T(8,128)S(1)}, u32[]{:S(2)}, u32[]{:S(2)}) collective-permute-start(f32[144,128]{1,0:T(8,128)S(1)} %pad_maximum_fusion.refs_3_), channel_id=1, source_target_pairs={{0,8},{8,16},{16,24},{24,32},{32,40},{40,48},{48,56},{56,64},{64,7... | collective-permute-start | bytes 221192 | tf_op jit(solution)/shard_map/ppermute | solution.py:31
  14.4 4.0 %collective-permute-start.3 = (f32[144,128]{1,0:T(8,128)S(1)}, f32[144,128]{1,0:T(8,128)S(1)}, u32[]{:S(2)}, u32[]{:S(2)}) collective-permute-start(f32[144,128]{1,0:T(8,128)S(1)} %pad_maximum_fusion.refs_3_), channel_id=1, source_target_pairs={{8,0},{16,8},{24,16},{32,24},{40,32},{48,40},{56,48},{64,56},{72,6... | collective-permute-start | bytes 221192 | tf_op jit(solution)/shard_map/ppermute | solution.py:31
  18.4 4.2 %collective-permute-start.4 = (f32[144,128]{1,0:T(8,128)S(1)}, f32[144,128]{1,0:T(8,128)S(1)}, u32[]{:S(2)}, u32[]{:S(2)}) collective-permute-start(f32[144,128]{1,0:T(8,128)S(1)} %pad_maximum_fusion.refs_3_), channel_id=1, source_target_pairs={{16,0},{24,8},{32,16},{40,24},{48,32},{56,40},{64,48},{72,56},{80,... | collective-permute-start | bytes 221192 | tf_op jit(solution)/shard_map/ppermute | solution.py:31
  22.6 0.7 copy-done.3
  23.4 3.1 %collective-permute-start.5 = (f32[144,128]{1,0:T(8,128)S(1)}, f32[144,128]{1,0:T(8,128)S(1)}, u32[]{:S(2)}, u32[]{:S(2)}) collective-permute-start(f32[144,128]{1,0:T(8,128)S(1)} %pad_maximum_fusion.refs_3_), channel_id=1, source_target_pairs={{24,0},{32,8},{40,16},{48,24},{56,32},{64,40},{72,48},{80,56},{88,... | collective-permute-start | bytes 221192 | tf_op jit(solution)/shard_map/ppermute | solution.py:31
  26.8 3.6 %collective-permute-done.5.refs_6_ = f32[144,128]{1,0:T(8,128)S(1)} collective-permute-done((f32[144,128]{1,0:T(8,128)S(1)}, f32[144,128]{1,0:T(8,128)S(1)}, u32[]{:S(2)}, u32[]{:S(2)}) %collective-permute-start.5) | collective-permute-done | bytes 73760 | tf_op jit(solution)/shard_map/ppermute | solution.py:31
  30.4 30.0 %farm.1 = (f32[16,1024]{1,0:T(8,128)}, f32[8,128]{1,0:T(8,128)S(1)}, f32[8,128]{1,0:T(8,128)S(1)}, f32[8,128]{1,0:T(8,128)S(1)}, f32[8,128]{1,0:T(8,128)S(1)}, /...) custom-call(s32[8,16]{1,0:T(8,128)S(1)} %bitcast_select_fusion.index_ref, ...), custom_call_target="tpu_custom_call" | custom-call | flops 1073741824 | bytes 4194304 | tf_op jit(solution)/shard_map/farm/pallas_call | solution.py:156
  60.4 7.7 %collective-permute-start.10 = (f32[8,128]{1,0:T(8,128)S(1)}, f32[8,128]{1,0:T(8,128)S(1)}, u32[]{:S(2)}, u32[]{:S(2)}) collective-permute-start(f32[8,128]{1,0:T(8,128)S(1)} %get-tuple-element.18), channel_id=1, source_target_pairs={{0,16},{8,24},{16,32},{24,40},{32,48},{40,56},{48,64},{56,72},{64,... | collective-permute-start | bytes 12296 | tf_op jit(solution)/shard_map/ppermute | solution.py:31
  68.1 1.9 %collective-permute-start.11 = (f32[8,128]{1,0:T(8,128)S(1)}, f32[8,128]{1,0:T(8,128)S(1)}, u32[]{:S(2)}, u32[]{:S(2)}) collective-permute-start(f32[8,128]{1,0:T(8,128)S(1)} %get-tuple-element.19), channel_id=1, source_target_pairs={{0,24},{8,32},{16,40},{24,48},{32,56},{40,64},{48,72},{56,80},{64,... | collective-permute-start | bytes 12296 | tf_op jit(solution)/shard_map/ppermute | solution.py:31
  70.0 6.7 %collective-permute-start.6 = (f32[8,128]{1,0:T(8,128)S(1)}, f32[8,128]{1,0:T(8,128)S(1)}, u32[]{:S(2)}, u32[]{:S(2)}) collective-permute-start(f32[8,128]{1,0:T(8,128)S(1)} %get-tuple-element.14), channel_id=1, source_target_pairs={{24,0},{32,8},{40,16},{48,24},{56,32},{64,40},{72,48},{80,56},{88,... | collective-permute-start | bytes 12296 | tf_op jit(solution)/shard_map/ppermute | solution.py:31
  76.7 5.1 %collective-permute-start.7 = (f32[8,128]{1,0:T(8,128)S(1)}, f32[8,128]{1,0:T(8,128)S(1)}, u32[]{:S(2)}, u32[]{:S(2)}) collective-permute-start(f32[8,128]{1,0:T(8,128)S(1)} %get-tuple-element.15), channel_id=1, source_target_pairs={{16,0},{24,8},{32,16},{40,24},{48,32},{56,40},{64,48},{72,56},{80,... | collective-permute-start | bytes 12296 | tf_op jit(solution)/shard_map/ppermute | solution.py:31
  81.8 3.4 %collective-permute-start.8 = (f32[8,128]{1,0:T(8,128)S(1)}, f32[8,128]{1,0:T(8,128)S(1)}, u32[]{:S(2)}, u32[]{:S(2)}) collective-permute-start(f32[8,128]{1,0:T(8,128)S(1)} %get-tuple-element.16), channel_id=1, source_target_pairs={{8,0},{16,8},{24,16},{32,24},{40,32},{48,40},{56,48},{64,56},{72,6... | collective-permute-start | bytes 12296 | tf_op jit(solution)/shard_map/ppermute | solution.py:31
  85.2 2.0 %collective-permute-start.9 = (f32[8,128]{1,0:T(8,128)S(1)}, f32[8,128]{1,0:T(8,128)S(1)}, u32[]{:S(2)}, u32[]{:S(2)}) collective-permute-start(f32[8,128]{1,0:T(8,128)S(1)} %get-tuple-element.17), channel_id=1, source_target_pairs={{0,8},{8,16},{16,24},{24,32},{32,40},{40,48},{48,56},{56,64},{64,7... | collective-permute-start | bytes 12296 | tf_op jit(solution)/shard_map/ppermute | solution.py:31
  87.3 5.0 %collective-permute-done.9 = f32[8,128]{1,0:T(8,128)S(1)} collective-permute-done((f32[8,128]{1,0:T(8,128)S(1)}, f32[8,128]{1,0:T(8,128)S(1)}, u32[]{:S(2)}, u32[]{:S(2)}) %collective-permute-start.9) | collective-permute-done | bytes 4128 | tf_op jit(solution)/shard_map/ppermute | solution.py:31
  92.3 1.9 %collective-permute-start.12 = (f32[8,128]{1,0:T(8,128)S(1)}, f32[8,128]{1,0:T(8,128)S(1)}, u32[]{:S(2)}, u32[]{:S(2)}) collective-permute-start(f32[8,128]{1,0:T(8,128)S(1)} %divide_add_fusion), channel_id=1, source_target_pairs={{0,1},{1,0},{2,3},{3,2},{4,5},{5,4},{6,7},{7,6},{8,9},{9,8},{10,11... | collective-permute-start | bytes 12296 | tf_op jit(solution)/shard_map/ppermute | solution.py:199
  94.2 3.6 %collective-permute-done.12 = f32[8,128]{1,0:T(8,128)S(1)} collective-permute-done((f32[8,128]{1,0:T(8,128)S(1)}, f32[8,128]{1,0:T(8,128)S(1)}, u32[]{:S(2)}, u32[]{:S(2)}) %collective-permute-start.12) | collective-permute-done | bytes 4128 | tf_op jit(solution)/shard_map/ppermute | solution.py:199
  97.8 1.9 %collective-permute-start.13 = (f32[8,128]{1,0:T(8,128)S(1)}, f32[8,128]{1,0:T(8,128)S(1)}, u32[]{:S(2)}, u32[]{:S(2)}) collective-permute-start(f32[8,128]{1,0:T(8,128)S(1)} %add.43), channel_id=1, source_target_pairs={{0,2},{1,3},{2,0},{3,1},{4,6},{5,7},{6,4},{7,5},{8,10},{9,11},{10,... | collective-permute-start | bytes 12296 | tf_op jit(solution)/shard_map/ppermute | solution.py:199
  99.7 4.5 %collective-permute-done.13 = f32[8,128]{1,0:T(8,128)S(1)} collective-permute-done((f32[8,128]{1,0:T(8,128)S(1)}, f32[8,128]{1,0:T(8,128)S(1)}, u32[]{:S(2)}, u32[]{:S(2)}) %collective-permute-start.13) | collective-permute-done | bytes 4128 | tf_op jit(solution)/shard_map/ppermute | solution.py:199
  104.2 1.9 %collective-permute-start.14 = (f32[8,128]{1,0:T(8,128)S(1)}, f32[8,128]{1,0:T(8,128)S(1)}, u32[]{:S(2)}, u32[]{:S(2)}) collective-permute-start(f32[8,128]{1,0:T(8,128)S(1)} %add.44), channel_id=1, source_target_pairs={{0,4},{1,5},{2,6},{3,7},{4,0},{5,1},{6,2},{7,3},{8,12},{9,13},{10,... | collective-permute-start | bytes 12296 | tf_op jit(solution)/shard_map/ppermute | solution.py:199
  106.1 7.5 %collective-permute-done.14 = f32[8,128]{1,0:T(8,128)S(1)} collective-permute-done((f32[8,128]{1,0:T(8,128)S(1)}, f32[8,128]{1,0:T(8,128)S(1)}, u32[]{:S(2)}, u32[]{:S(2)}) %collective-permute-start.14) | collective-permute-done | bytes 4128 | tf_op jit(solution)/shard_map/ppermute | solution.py:199
  (33 shorter events, 1.1 us)
Async XLA Ops:
  0.6 0.9 copy-start
  1.5 0.7 copy-start.2
  1.5 0.7 copy-start.1
  2.2 21.1 %collective-permute-start = (f32[144,128]{1,0:T(8,128)S(1)}, f32[144,128]{1,0:T(8,128)S(1)}, u32[]{:S(2)}, u32[]{:S(2)}) collective-permute-start(f32[144,128]{1,0:T(8,128)S(1)} %pad_maximum_fusion.refs_3_), channel_id=1, source_target_pairs={{0,24},{8,32},{16,40},{24,48},{32,56},{40,64},{48,72},{56,80},{64,... | collective-permute-start | bytes 221192 | tf_op jit(solution)/shard_map/ppermute | solution.py:31
  6.0 20.8 %collective-permute-start.1 = (f32[144,128]{1,0:T(8,128)S(1)}, f32[144,128]{1,0:T(8,128)S(1)}, u32[]{:S(2)}, u32[]{:S(2)}) collective-permute-start(f32[144,128]{1,0:T(8,128)S(1)} %pad_maximum_fusion.refs_3_), channel_id=1, source_target_pairs={{0,16},{8,24},{16,32},{24,40},{32,48},{40,56},{48,64},{56,72},{64,... | collective-permute-start | bytes 221192 | tf_op jit(solution)/shard_map/ppermute | solution.py:31
  10.2 16.5 %collective-permute-start.2 = (f32[144,128]{1,0:T(8,128)S(1)}, f32[144,128]{1,0:T(8,128)S(1)}, u32[]{:S(2)}, u32[]{:S(2)}) collective-permute-start(f32[144,128]{1,0:T(8,128)S(1)} %pad_maximum_fusion.refs_3_), channel_id=1, source_target_pairs={{0,8},{8,16},{16,24},{24,32},{32,40},{40,48},{48,56},{56,64},{64,7... | collective-permute-start | bytes 221192 | tf_op jit(solution)/shard_map/ppermute | solution.py:31
  14.4 12.4 %collective-permute-start.3 = (f32[144,128]{1,0:T(8,128)S(1)}, f32[144,128]{1,0:T(8,128)S(1)}, u32[]{:S(2)}, u32[]{:S(2)}) collective-permute-start(f32[144,128]{1,0:T(8,128)S(1)} %pad_maximum_fusion.refs_3_), channel_id=1, source_target_pairs={{8,0},{16,8},{24,16},{32,24},{40,32},{48,40},{56,48},{64,56},{72,6... | collective-permute-start | bytes 221192 | tf_op jit(solution)/shard_map/ppermute | solution.py:31
  18.4 8.4 %collective-permute-start.4 = (f32[144,128]{1,0:T(8,128)S(1)}, f32[144,128]{1,0:T(8,128)S(1)}, u32[]{:S(2)}, u32[]{:S(2)}) collective-permute-start(f32[144,128]{1,0:T(8,128)S(1)} %pad_maximum_fusion.refs_3_), channel_id=1, source_target_pairs={{16,0},{24,8},{32,16},{40,24},{48,32},{56,40},{64,48},{72,56},{80,... | collective-permute-start | bytes 221192 | tf_op jit(solution)/shard_map/ppermute | solution.py:31
  22.6 0.7 copy-start.3
  22.6 0.7 copy-start.4
  23.4 7.0 %collective-permute-start.5 = (f32[144,128]{1,0:T(8,128)S(1)}, f32[144,128]{1,0:T(8,128)S(1)}, u32[]{:S(2)}, u32[]{:S(2)}) collective-permute-start(f32[144,128]{1,0:T(8,128)S(1)} %pad_maximum_fusion.refs_3_), channel_id=1, source_target_pairs={{24,0},{32,8},{40,16},{48,24},{56,32},{64,40},{72,48},{80,56},{88,... | collective-permute-start | bytes 221192 | tf_op jit(solution)/shard_map/ppermute | solution.py:31
  26.7 3.6 %copy-start.5 = (f32[1,16]{1,0:T(1,128)S(1)}, f32[1,16]{1,0:T(1,128)}, u32[]{:S(2)}) copy-start(f32[1,16]{1,0:T(1,128)} %param.11) | copy-start | bytes 196
  60.4 24.8 %collective-permute-start.10 = (f32[8,128]{1,0:T(8,128)S(1)}, f32[8,128]{1,0:T(8,128)S(1)}, u32[]{:S(2)}, u32[]{:S(2)}) collective-permute-start(f32[8,128]{1,0:T(8,128)S(1)} %get-tuple-element.18), channel_id=1, source_target_pairs={{0,16},{8,24},{16,32},{24,40},{32,48},{40,56},{48,64},{56,72},{64,... | collective-permute-start | bytes 12296 | tf_op jit(solution)/shard_map/ppermute | solution.py:31
  68.1 19.1 %collective-permute-start.11 = (f32[8,128]{1,0:T(8,128)S(1)}, f32[8,128]{1,0:T(8,128)S(1)}, u32[]{:S(2)}, u32[]{:S(2)}) collective-permute-start(f32[8,128]{1,0:T(8,128)S(1)} %get-tuple-element.19), channel_id=1, source_target_pairs={{0,24},{8,32},{16,40},{24,48},{32,56},{40,64},{48,72},{56,80},{64,... | collective-permute-start | bytes 12296 | tf_op jit(solution)/shard_map/ppermute | solution.py:31
  70.0 17.2 %collective-permute-start.6 = (f32[8,128]{1,0:T(8,128)S(1)}, f32[8,128]{1,0:T(8,128)S(1)}, u32[]{:S(2)}, u32[]{:S(2)}) collective-permute-start(f32[8,128]{1,0:T(8,128)S(1)} %get-tuple-element.14), channel_id=1, source_target_pairs={{24,0},{32,8},{40,16},{48,24},{56,32},{64,40},{72,48},{80,56},{88,... | collective-permute-start | bytes 12296 | tf_op jit(solution)/shard_map/ppermute | solution.py:31
  76.7 10.6 %collective-permute-start.7 = (f32[8,128]{1,0:T(8,128)S(1)}, f32[8,128]{1,0:T(8,128)S(1)}, u32[]{:S(2)}, u32[]{:S(2)}) collective-permute-start(f32[8,128]{1,0:T(8,128)S(1)} %get-tuple-element.15), channel_id=1, source_target_pairs={{16,0},{24,8},{32,16},{40,24},{48,32},{56,40},{64,48},{72,56},{80,... | collective-permute-start | bytes 12296 | tf_op jit(solution)/shard_map/ppermute | solution.py:31
  81.8 5.4 %collective-permute-start.8 = (f32[8,128]{1,0:T(8,128)S(1)}, f32[8,128]{1,0:T(8,128)S(1)}, u32[]{:S(2)}, u32[]{:S(2)}) collective-permute-start(f32[8,128]{1,0:T(8,128)S(1)} %get-tuple-element.16), channel_id=1, source_target_pairs={{8,0},{16,8},{24,16},{32,24},{40,32},{48,40},{56,48},{64,56},{72,6... | collective-permute-start | bytes 12296 | tf_op jit(solution)/shard_map/ppermute | solution.py:31
  85.2 7.0 %collective-permute-start.9 = (f32[8,128]{1,0:T(8,128)S(1)}, f32[8,128]{1,0:T(8,128)S(1)}, u32[]{:S(2)}, u32[]{:S(2)}) collective-permute-start(f32[8,128]{1,0:T(8,128)S(1)} %get-tuple-element.17), channel_id=1, source_target_pairs={{0,8},{8,16},{16,24},{24,32},{32,40},{40,48},{48,56},{56,64},{64,7... | collective-permute-start | bytes 12296 | tf_op jit(solution)/shard_map/ppermute | solution.py:31
  92.3 5.5 %collective-permute-start.12 = (f32[8,128]{1,0:T(8,128)S(1)}, f32[8,128]{1,0:T(8,128)S(1)}, u32[]{:S(2)}, u32[]{:S(2)}) collective-permute-start(f32[8,128]{1,0:T(8,128)S(1)} %divide_add_fusion), channel_id=1, source_target_pairs={{0,1},{1,0},{2,3},{3,2},{4,5},{5,4},{6,7},{7,6},{8,9},{9,8},{10,11... | collective-permute-start | bytes 12296 | tf_op jit(solution)/shard_map/ppermute | solution.py:199
  97.8 6.4 %collective-permute-start.13 = (f32[8,128]{1,0:T(8,128)S(1)}, f32[8,128]{1,0:T(8,128)S(1)}, u32[]{:S(2)}, u32[]{:S(2)}) collective-permute-start(f32[8,128]{1,0:T(8,128)S(1)} %add.43), channel_id=1, source_target_pairs={{0,2},{1,3},{2,0},{3,1},{4,6},{5,7},{6,4},{7,5},{8,10},{9,11},{10,... | collective-permute-start | bytes 12296 | tf_op jit(solution)/shard_map/ppermute | solution.py:199
  104.2 9.4 %collective-permute-start.14 = (f32[8,128]{1,0:T(8,128)S(1)}, f32[8,128]{1,0:T(8,128)S(1)}, u32[]{:S(2)}, u32[]{:S(2)}) collective-permute-start(f32[8,128]{1,0:T(8,128)S(1)} %add.44), channel_id=1, source_target_pairs={{0,4},{1,5},{2,6},{3,7},{4,0},{5,1},{6,2},{7,3},{8,12},{9,13},{10,... | collective-permute-start | bytes 12296 | tf_op jit(solution)/shard_map/ppermute | solution.py:199

commit v2 on v1

--- a/solution.py
+++ b/solution.py
@@ -13,6 +13,7 @@
 SPEEDS = 16
 REACH = 3
 PIECES = 2 * REACH + 1
+GROUP = 8
 SOURCES = PIECES * BLKS
 NULL = SOURCES
 PAIRS = 16
@@ -53,12 +54,11 @@
     return base + [k * u1 for k in base] + [k * u4 for k in base]
 
 
-def farm_kernel(index_ref, pairs_ref, *refs):
+def farm_kernel(index_ref, pairs_ref, place_ref, *refs):
     pieces = refs[:PIECES]
     axial_ref, spread_ref, freq_ref = refs[PIECES : PIECES + 3]
-    power_ref, direct_ref = refs[PIECES + 3 : PIECES + 5]
-    back_refs = refs[PIECES + 5 : 2 * PIECES + 5]
-    s_ref, xs_ref, ys_ref, xt_ref, yt_ref, d_ref, a_ref, k_ref, b_ref = refs[2 * PIECES + 5 :]
+    power_ref, direct_ref, send_ref = refs[PIECES + 3 : PIECES + 6]
+    s_ref, xs_ref, ys_ref, xt_ref, yt_ref, d_ref, a_ref, k_ref, b_ref, g_ref = refs[PIECES + 6 :]
 
     for o in range(PIECES):
         for blk in range(BLKS):
@@ -94,16 +94,15 @@
             strength = jnp.concatenate([s_ref[q0], s_ref[q1]], axis=1)
             sx = [jnp.concatenate([xs_ref[q]] * 2, axis=0) for q in (q0, q1)]
             sy = [jnp.concatenate([ys_ref[q]] * 2, axis=0) for q in (q0, q1)]
-            zero = jnp.zeros((ROWS, 2 * BLOCK), jnp.bfloat16)
+            zero = jnp.zeros((ROWS, BLOCK), jnp.bfloat16)
             for tc in range(CHUNKS):
                 tx = xt_ref[tc * ROWS : (tc + 1) * ROWS, :]
                 ty = yt_ref[tc * ROWS : (tc + 1) * ROWS, :]
                 halves = [wake_tiles(tx, ty, sx[h], sy[h]) for h in range(2)]
-                kernel = jnp.concatenate(
-                    [jnp.concatenate([k0.astype(jnp.bfloat16), k1.astype(jnp.bfloat16)], axis=1) for k0, k1 in zip(*halves)] + [zero],
-                    axis=0,
-                )
-                k_ref[p, tc * LANES : (tc + 1) * LANES, :] = kernel
+                columns = [jnp.concatenate([k.astype(jnp.bfloat16) for k in half] + [zero], axis=0) for half in halves]
+                for h in range(2):
+                    k_ref[p, h, tc * LANES : (tc + 1) * LANES, :] = columns[h]
+                kernel = jnp.concatenate(columns, axis=1)
                 d_ref[tc] += lax.dot_general(strength, kernel, (((1,), (1,)), ((), ())), preferred_element_type=jnp.float32)
             return carry
 
@@ -131,7 +130,8 @@
         direct_ref[pl.ds(b, 1), :] = jnp.sum(freq * (slope_coef * cube), axis=0, keepdims=True)
 
         def backward(p, carry):
-            term = jnp.dot(a_ref[...], k_ref[p], preferred_element_type=jnp.float32)
+            kernel = jnp.concatenate([k_ref[p, 0], k_ref[p, 1]], axis=1)
+            term = jnp.dot(a_ref[...], kernel, preferred_element_type=jnp.float32)
             b_ref[index_ref[b, 2 * p]] += term[:, :BLOCK]
             b_ref[index_ref[b, 2 * p + 1]] += term[:, BLOCK:]
             return carry
@@ -145,10 +145,22 @@
         for blk in range(BLKS):
             strength = pieces[o][blk * SPEEDS : (blk + 1) * SPEEDS, :]
             rows.append(jnp.sum(freq * strength * b_ref[o * BLKS + blk], axis=0, keepdims=True))
-        back_refs[o][...] = jnp.concatenate(rows, axis=0)
-
-
-def farm(index, pairs, pieces, axial, spread, freq):
+        g_ref[GROUP - 1 + o] = jnp.concatenate(rows, axis=0)
+    for o in list(range(GROUP - 1)) + list(range(GROUP - 1 + PIECES, 2 * GROUP + PIECES - 2)):
+        g_ref[o] = jnp.zeros((BLKS, BLOCK), jnp.float32)
+    place = place_ref[0]
+    for i in range(GROUP):
+        first = i - place + GROUP - 1
+        send_ref[i, 0] = g_ref[first + REACH]
+        if i < REACH:
+            send_ref[i, 1] = g_ref[first]
+        elif i >= GROUP - REACH:
+            send_ref[i, 1] = g_ref[first + 2 * REACH]
+        else:
+            send_ref[i, 1] = jnp.zeros((BLKS, BLOCK), jnp.float32)
+
+
+def farm(index, pairs, place, pieces, axial, spread, freq):
     f32 = jnp.float32
     smem = pl.BlockSpec(memory_space=pltpu.SMEM)
     vmem = pl.BlockSpec(memory_space=pltpu.VMEM)
@@ -156,9 +168,9 @@
     return pl.pallas_call(
         farm_kernel,
         name="farm",
-        out_shape=(jax.ShapeDtypeStruct((SPEEDS, BLKS * BLOCK), f32), piece) + (piece,) * PIECES,
-        in_specs=[smem, smem] + [vmem] * (PIECES + 3),
-        out_specs=(vmem,) * (PIECES + 2),
+        out_shape=(jax.ShapeDtypeStruct((SPEEDS, BLKS * BLOCK), f32), piece, jax.ShapeDtypeStruct((GROUP, 2, BLKS, BLOCK), f32)),
+        in_specs=[smem, smem, smem] + [vmem] * (PIECES + 3),
+        out_specs=(vmem,) * 3,
         scratch_shapes=[
             pltpu.VMEM((SOURCES + 1, SPEEDS, BLOCK), jnp.bfloat16),
             pltpu.VMEM((SOURCES + 1, 8, BLOCK), f32),
@@ -167,12 +179,13 @@
             pltpu.VMEM((BLOCK, BLOCK), f32),
             pltpu.VMEM((CHUNKS, SPEEDS, LANES), f32),
             pltpu.VMEM((SPEEDS, CHUNKS * LANES), jnp.bfloat16),
-            pltpu.VMEM((PAIRS // 2, CHUNKS * LANES, 2 * BLOCK), jnp.bfloat16),
+            pltpu.VMEM((PAIRS // 2, 2, CHUNKS * LANES, BLOCK), jnp.bfloat16),
             pltpu.VMEM((SOURCES + 1, SPEEDS, BLOCK), f32),
+            pltpu.VMEM((2 * GROUP + PIECES - 2, BLKS, BLOCK), f32),
         ],
         compiler_params=pltpu.CompilerParams(vmem_limit_bytes=32 << 20),
         cost_estimate=pl.CostEstimate(flops=2 * 64 * 128 * 2048 * 16 * 2, bytes_accessed=4 << 20, transcendentals=0),
-    )(index, pairs, *pieces, axial, spread, freq)
+    )(index, pairs, place, *pieces, axial, spread, freq)
 
 
 def body(axial, thrust_weight, xdown, ycross, freq, upstream, counts):
@@ -189,14 +202,19 @@
     power_coef = 4.0 * axial_rows * (1.0 - axial_rows) ** 2
     spread = jnp.broadcast_to(power_coef.reshape(BLKS, CHUNKS, 1, ROWS), (BLKS, CHUNKS, BLOCK // ROWS, ROWS)).reshape(BLKS, CHUNKS, BLOCK)
     freq_wide = jnp.broadcast_to(freq[0][:, None], (SPEEDS, BLOCK))
-    power, direct, *back = farm(index, pairs, pieces, axial_rows, spread, freq_wide)
-    total = back[REACH]
-    for o in range(PIECES):
-        if o != REACH:
-            total = total + from_behind(back[o], "pt", o - REACH)
+    place = (position % GROUP).reshape(1)
+    power, direct, send = farm(index, pairs, place, pieces, axial_rows, spread, freq_wide)
+    length = lax.axis_size("pt")
+    groups = [list(range(a, a + GROUP)) for a in range(0, length, GROUP)]
+    arrived = jnp.sum(lax.all_to_all(send, "pt", 0, 0, axis_index_groups=groups), axis=0)
+    across = []
+    for a in range(GROUP, length, GROUP):
+        for i in range(REACH):
+            across += [(a - REACH + i, a + i), (a + i, a - REACH + i)]
+    total = arrived[0] + lax.ppermute(arrived[1], "pt", across)
     gradient = direct + total / axial_rows
-    for bit in (1, 2, 4):
-        gradient = gradient + lax.ppermute(gradient, "dir", [(i, i ^ bit) for i in range(lax.axis_size("dir"))])
+    spread_out = jnp.broadcast_to(gradient[None], (lax.axis_size("dir"),) + gradient.shape)
+    gradient = jnp.sum(lax.all_to_all(spread_out, "dir", 0, 0), axis=0)
     return power[None], gradient.reshape(-1)
 
 

time: 115 us -> 104 us (0.904)
  the two profiles are of different devices: /device:TPU:18 before, /device:TPU:2 now
where the time goes in v2:
time: 104 us; the launch traced here: 103 us
  blocking collectives  41.2 us (40%)
  starting transfers between devices  40.4 us (39%)
  Pallas kernels  12.1 us (12%)
  waiting for transfers between devices  4.89 us (5%)
  local copies, waits for them, and re-layouts  3.17 us (3%)
    all_to_all x1, blocking collectives, body(): gradient = jnp.sum(lax.all_to_all(spread_out, 'dir', 0, 0), axis=0)  30.1 us
    ppermute x6, starting transfers between devices, from_behind(): return lax.ppermute(value, axis, pairs)  23.4 us
    ppermute x1, starting transfers between devices, body(): total = arrived[0] + lax.ppermute(arrived[1], 'pt', across)  17 us
    pallas_call x1, Pallas kernels, farm(): pl.pallas_call(farm_kernel, name='farm', out_shape=(jax.ShapeDtypeStruct(...  12.1 us
    all_to_all x1, blocking collectives, body(): lax.all_to_all(send, 'pt', 0, 0, axis_index_groups=groups)  11 us
    ppermute x6, waiting for transfers between devices, from_behind(): return lax.ppermute(value, axis, pairs)  3.58 us
    unnamed x13, local copies, waits for them, and re-layouts  2.88 us
  transfers between devices with their start and end apart: 7, of which 2 were waited for; matrix products, arithmetic and copies ran while one was open for 0% of the time, Pallas kernels for 0%

profile of v2, /device:TPU:2, one launch (start us, length us, event | category | flops | bytes accessed | tf_op | source)
XLA Modules:
  0.0 103.3 jit_solution(14314982250059593634)
XLA Ops:
  0.6 0.9 copy.11
  1.5 0.0 copy-start.1
  1.6 0.6 copy-done.2
  2.2 0.0 copy-done.1
  2.2 3.7 %collective-permute-start = (f32[144,128]{1,0:T(8,128)S(1)}, f32[144,128]{1,0:T(8,128)S(1)}, u32[]{:S(2)}, u32[]{:S(2)}) collective-permute-start(f32[144,128]{1,0:T(8,128)S(1)} %pad_maximum_fusion.refs_3_), channel_id=1, source_target_pairs={{0,24},{8,32},{16,40},{24,48},{32,56},{40,64},{48,72},{56,80},{64,... | collective-permute-start | bytes 221192 | tf_op jit(solution)/shard_map/ppermute | solution.py:32
  6.0 4.3 %collective-permute-start.1 = (f32[144,128]{1,0:T(8,128)S(1)}, f32[144,128]{1,0:T(8,128)S(1)}, u32[]{:S(2)}, u32[]{:S(2)}) collective-permute-start(f32[144,128]{1,0:T(8,128)S(1)} %pad_maximum_fusion.refs_3_), channel_id=1, source_target_pairs={{0,16},{8,24},{16,32},{24,40},{32,48},{40,56},{48,64},{56,72},{64,... | collective-permute-start | bytes 221192 | tf_op jit(solution)/shard_map/ppermute | solution.py:32
  10.2 4.1 %collective-permute-start.2 = (f32[144,128]{1,0:T(8,128)S(1)}, f32[144,128]{1,0:T(8,128)S(1)}, u32[]{:S(2)}, u32[]{:S(2)}) collective-permute-start(f32[144,128]{1,0:T(8,128)S(1)} %pad_maximum_fusion.refs_3_), channel_id=1, source_target_pairs={{0,8},{8,16},{16,24},{24,32},{32,40},{40,48},{48,56},{56,64},{64,7... | collective-permute-start | bytes 221192 | tf_op jit(solution)/shard_map/ppermute | solution.py:32
  14.4 4.0 %collective-permute-start.3 = (f32[144,128]{1,0:T(8,128)S(1)}, f32[144,128]{1,0:T(8,128)S(1)}, u32[]{:S(2)}, u32[]{:S(2)}) collective-permute-start(f32[144,128]{1,0:T(8,128)S(1)} %pad_maximum_fusion.refs_3_), channel_id=1, source_target_pairs={{8,0},{16,8},{24,16},{32,24},{40,32},{48,40},{56,48},{64,56},{72,6... | collective-permute-start | bytes 221192 | tf_op jit(solution)/shard_map/ppermute | solution.py:32
  18.4 4.2 %collective-permute-start.4 = (f32[144,128]{1,0:T(8,128)S(1)}, f32[144,128]{1,0:T(8,128)S(1)}, u32[]{:S(2)}, u32[]{:S(2)}) collective-permute-start(f32[144,128]{1,0:T(8,128)S(1)} %pad_maximum_fusion.refs_3_), channel_id=1, source_target_pairs={{16,0},{24,8},{32,16},{40,24},{48,32},{56,40},{64,48},{72,56},{80,... | collective-permute-start | bytes 221192 | tf_op jit(solution)/shard_map/ppermute | solution.py:32
  22.6 0.0 copy-start.3
  22.6 0.7 copy-done.3
  23.3 0.1 bitcast_select_fusion.index_ref
  23.4 3.1 %collective-permute-start.5 = (f32[144,128]{1,0:T(8,128)S(1)}, f32[144,128]{1,0:T(8,128)S(1)}, u32[]{:S(2)}, u32[]{:S(2)}) collective-permute-start(f32[144,128]{1,0:T(8,128)S(1)} %pad_maximum_fusion.refs_3_), channel_id=1, source_target_pairs={{24,0},{32,8},{40,16},{48,24},{56,32},{64,40},{72,48},{80,56},{88,... | collective-permute-start | bytes 221192 | tf_op jit(solution)/shard_map/ppermute | solution.py:32
  26.5 0.1 mul.42
  26.6 0.1 reshape.50.refs_8_
  26.8 3.6 %collective-permute-done.5.refs_6_ = f32[144,128]{1,0:T(8,128)S(1)} collective-permute-done((f32[144,128]{1,0:T(8,128)S(1)}, f32[144,128]{1,0:T(8,128)S(1)}, u32[]{:S(2)}, u32[]{:S(2)}) %collective-permute-start.5) | collective-permute-done | bytes 73760 | tf_op jit(solution)/shard_map/ppermute | solution.py:32
  30.3 0.7 copy-done.5
  31.0 0.1 broadcast_in_dim.29.refs_9_
  31.1 12.1 %farm.1 = (f32[16,1024]{1,0:T(8,128)}, f32[8,128]{1,0:T(8,128)S(1)}, f32[8,2,8,128]{3,2,1,0:T(8,128)S(1)}) custom-call(s32[8,16]{1,0:T(8,128)S(1)} %bitcast_select_fusion.index_ref, s32[8]{0:T(128)S(1)} %and_select_fusion.pairs_ref, s32[1]{0:T(128)} %bitcast.2.place_ref, f32[144,128]{1,0:T(8,128)S(1)} %collective-permute-done.refs_0_, ...), custom_call_target="tpu_custom_call" | custom-call | flops 1073741824 | bytes 4194304 | tf_op jit(solution)/shard_map/farm/pallas_call | solution.py:168
  43.1 11.0 %all_to_all.10 = f32[8,2,8,128]{3,2,1,0:T(8,128)S(1)} all-to-all(f32[8,2,8,128]{3,2,1,0:T(8,128)S(1)} %get-tuple-element.7), channel_id=1, replica_groups={{0,8,16,24,32,40,48,56},{64,72,80,88,96,104,112,120},{128,136,144,152,1..., dimensions={0} | all-to-all | bytes 131072 | tf_op jit(solution)/shard_map/all_to_all | solution.py:209
  54.2 17.0 %collective-permute-start.6 = (f32[8,128]{1,0:T(8,128)S(1)}, f32[8,128]{1,0:T(8,128)S(1)}, u32[]{:S(2)}, u32[]{:S(2)}) collective-permute-start(f32[8,128]{1,0:T(8,128)S(1)} %slice_bitcast_fusion), channel_id=1, source_target_pairs={{40,64},{64,40},{48,72},{72,48},{56,80},{80,56},{104,128},{128,104... | collective-permute-start | bytes 12296 | tf_op jit(solution)/shard_map/ppermute | solution.py:214
  71.2 1.3 %collective-permute-done.6 = f32[8,128]{1,0:T(8,128)S(1)} collective-permute-done((f32[8,128]{1,0:T(8,128)S(1)}, f32[8,128]{1,0:T(8,128)S(1)}, u32[]{:S(2)}, u32[]{:S(2)}) %collective-permute-start.6) | collective-permute-done | bytes 4128 | tf_op jit(solution)/shard_map/ppermute | solution.py:214
  72.5 30.1 %all_to_all.11 = f32[8,8,128]{2,1,0:T(8,128)S(1)} all-to-all(f32[8,8,128]{2,1,0:T(8,128)S(1)} %broadcast_in_dim.31), channel_id=1, replica_groups=mesh['pt'=64,'dir'=8] {'dir'}, dimensions={0} | all-to-all | bytes 65536 | tf_op jit(solution)/shard_map/all_to_all | solution.py:217
  102.7 0.6 reduce_sum.19
  (20 shorter events, 0.1 us)
Async XLA Ops:
  0.6 0.9 copy-start
  1.5 0.7 copy-start.2
  1.5 0.7 copy-start.1
  2.2 21.1 %collective-permute-start = (f32[144,128]{1,0:T(8,128)S(1)}, f32[144,128]{1,0:T(8,128)S(1)}, u32[]{:S(2)}, u32[]{:S(2)}) collective-permute-start(f32[144,128]{1,0:T(8,128)S(1)} %pad_maximum_fusion.refs_3_), channel_id=1, source_target_pairs={{0,24},{8,32},{16,40},{24,48},{32,56},{40,64},{48,72},{56,80},{64,... | collective-permute-start | bytes 221192 | tf_op jit(solution)/shard_map/ppermute | solution.py:32
  6.0 20.8 %collective-permute-start.1 = (f32[144,128]{1,0:T(8,128)S(1)}, f32[144,128]{1,0:T(8,128)S(1)}, u32[]{:S(2)}, u32[]{:S(2)}) collective-permute-start(f32[144,128]{1,0:T(8,128)S(1)} %pad_maximum_fusion.refs_3_), channel_id=1, source_target_pairs={{0,16},{8,24},{16,32},{24,40},{32,48},{40,56},{48,64},{56,72},{64,... | collective-permute-start | bytes 221192 | tf_op jit(solution)/shard_map/ppermute | solution.py:32
  10.2 16.5 %collective-permute-start.2 = (f32[144,128]{1,0:T(8,128)S(1)}, f32[144,128]{1,0:T(8,128)S(1)}, u32[]{:S(2)}, u32[]{:S(2)}) collective-permute-start(f32[144,128]{1,0:T(8,128)S(1)} %pad_maximum_fusion.refs_3_), channel_id=1, source_target_pairs={{0,8},{8,16},{16,24},{24,32},{32,40},{40,48},{48,56},{56,64},{64,7... | collective-permute-start | bytes 221192 | tf_op jit(solution)/shard_map/ppermute | solution.py:32
  14.4 12.4 %collective-permute-start.3 = (f32[144,128]{1,0:T(8,128)S(1)}, f32[144,128]{1,0:T(8,128)S(1)}, u32[]{:S(2)}, u32[]{:S(2)}) collective-permute-start(f32[144,128]{1,0:T(8,128)S(1)} %pad_maximum_fusion.refs_3_), channel_id=1, source_target_pairs={{8,0},{16,8},{24,16},{32,24},{40,32},{48,40},{56,48},{64,56},{72,6... | collective-permute-start | bytes 221192 | tf_op jit(solution)/shard_map/ppermute | solution.py:32
  18.4 8.4 %collective-permute-start.4 = (f32[144,128]{1,0:T(8,128)S(1)}, f32[144,128]{1,0:T(8,128)S(1)}, u32[]{:S(2)}, u32[]{:S(2)}) collective-permute-start(f32[144,128]{1,0:T(8,128)S(1)} %pad_maximum_fusion.refs_3_), channel_id=1, source_target_pairs={{16,0},{24,8},{32,16},{40,24},{48,32},{56,40},{64,48},{72,56},{80,... | collective-permute-start | bytes 221192 | tf_op jit(solution)/shard_map/ppermute | solution.py:32
  22.6 0.7 copy-start.3
  22.6 0.7 copy-start.4
  23.4 7.0 %collective-permute-start.5 = (f32[144,128]{1,0:T(8,128)S(1)}, f32[144,128]{1,0:T(8,128)S(1)}, u32[]{:S(2)}, u32[]{:S(2)}) collective-permute-start(f32[144,128]{1,0:T(8,128)S(1)} %pad_maximum_fusion.refs_3_), channel_id=1, source_target_pairs={{24,0},{32,8},{40,16},{48,24},{56,32},{64,40},{72,48},{80,56},{88,... | collective-permute-start | bytes 221192 | tf_op jit(solution)/shard_map/ppermute | solution.py:32
  30.3 0.7 copy-start.5
  54.2 18.3 %collective-permute-start.6 = (f32[8,128]{1,0:T(8,128)S(1)}, f32[8,128]{1,0:T(8,128)S(1)}, u32[]{:S(2)}, u32[]{:S(2)}) collective-permute-start(f32[8,128]{1,0:T(8,128)S(1)} %slice_bitcast_fusion), channel_id=1, source_target_pairs={{40,64},{64,40},{48,72},{72,48},{56,80},{80,56},{104,128},{128,104... | collective-permute-start | bytes 12296 | tf_op jit(solution)/shard_map/ppermute | solution.py:214

commit v3 on v2

--- a/solution.py
+++ b/solution.py
@@ -24,12 +24,6 @@
 Y_SCALE = math.sqrt(2.0 * LOG2E)
 STEP = 0.2 * Y_SCALE
 WIDEN = 0.06 / LOG2E
-
-
-def from_behind(value, axis, by):
-    length = lax.axis_size(axis)
-    pairs = [(i, i + by) for i in range(length) if 0 <= i + by < length]
-    return lax.ppermute(value, axis, pairs)
 
 
 def wake_tiles(target_x, target_y, source_x, source_y):
@@ -145,7 +139,7 @@
         for blk in range(BLKS):
             strength = pieces[o][blk * SPEEDS : (blk + 1) * SPEEDS, :]
             rows.append(jnp.sum(freq * strength * b_ref[o * BLKS + blk], axis=0, keepdims=True))
-        g_ref[GROUP - 1 + o] = jnp.concatenate(rows, axis=0)
+        g_ref[GROUP - 1 + jnp.where(place_ref[1] == 0, o, PIECES - 1 - o)] = jnp.concatenate(rows, axis=0)
     for o in list(range(GROUP - 1)) + list(range(GROUP - 1 + PIECES, 2 * GROUP + PIECES - 2)):
         g_ref[o] = jnp.zeros((BLKS, BLOCK), jnp.float32)
     place = place_ref[0]
@@ -194,17 +188,25 @@
     strength = (axial[None, :] * thrust_weight[0]).reshape(SPEEDS, BLKS, BLOCK)
     strength = jnp.transpose(strength, (1, 0, 2)).reshape(BLKS * SPEEDS, BLOCK)
     packed = jnp.concatenate([strength, xdown[0].reshape(BLKS, BLOCK), ycross[0].reshape(BLKS, BLOCK)], axis=0)
-    pieces = [packed if o == REACH else from_behind(packed, "pt", REACH - o) for o in range(PIECES)]
+    length = lax.axis_size("pt")
+    core = position % 2
+    swap = [(i, i ^ 1) for i in range(length)]
+    hops = [[(i, i + by if i % 2 == up else i - by) for i in range(length)] for by, up in ((1, 1), (2, 0), (3, 1))]
+    hops = [[(i, j) for i, j in pairs if 0 <= j < length] for pairs in hops]
+    near, middle, far = [lax.ppermute(packed, "pt", pairs) for pairs in hops]
+    turned = [lax.ppermute(value, "pt", swap) for value in (packed, near, middle)]
+    pieces = [far, middle, near, packed] + turned
     slots = lax.broadcasted_iota(jnp.int32, (BLKS, PAIRS), 1)
-    index = jnp.where(slots < counts[0][:, None], upstream[0] - lowest, NULL)
+    local = upstream[0] - lowest
+    local = jnp.where(core == 0, local, (PIECES - 1) * BLKS - local + 2 * (local % BLKS))
+    index = jnp.where(slots < counts[0][:, None], local, NULL)
     pairs = (counts[0] + 1) // 2
     axial_rows = axial.reshape(BLKS, BLOCK)
     power_coef = 4.0 * axial_rows * (1.0 - axial_rows) ** 2
     spread = jnp.broadcast_to(power_coef.reshape(BLKS, CHUNKS, 1, ROWS), (BLKS, CHUNKS, BLOCK // ROWS, ROWS)).reshape(BLKS, CHUNKS, BLOCK)
     freq_wide = jnp.broadcast_to(freq[0][:, None], (SPEEDS, BLOCK))
-    place = (position % GROUP).reshape(1)
+    place = jnp.stack([position % GROUP, core])
     power, direct, send = farm(index, pairs, place, pieces, axial_rows, spread, freq_wide)
-    length = lax.axis_size("pt")
     groups = [list(range(a, a + GROUP)) for a in range(0, length, GROUP)]
     arrived = jnp.sum(lax.all_to_all(send, "pt", 0, 0, axis_index_groups=groups), axis=0)
     across = []

time: 104 us -> 97.2 us (0.935)
  the two profiles are of different devices: /device:TPU:2 before, /device:TPU:6 now
where the time goes in v3:
time: 97.2 us; the launch traced here: 96.7 us
  starting transfers between devices  41.7 us (43%)
  blocking collectives  28.7 us (30%)
  Pallas kernels  19.7 us (20%)
  local copies, waits for them, and re-layouts  2.52 us (3%)
  waiting for transfers between devices  2.45 us (3%)
    all_to_all x1, blocking collectives, body(): gradient = jnp.sum(lax.all_to_all(spread_out, 'dir', 0, 0), axis=0)  20.4 us
    pallas_call x1, Pallas kernels, farm(): pl.pallas_call(farm_kernel, name='farm', out_shape=(jax.ShapeDtypeStruct(...  19.7 us
    ppermute x1, starting transfers between devices, body(): total = arrived[0] + lax.ppermute(arrived[1], 'pt', across)  19 us
    ppermute x3, starting transfers between devices, body(): near, middle, far = [lax.ppermute(packed, 'pt', pairs) for pairs in hops]  16.5 us
    all_to_all x1, blocking collectives, body(): lax.all_to_all(send, 'pt', 0, 0, axis_index_groups=groups)  8.28 us
    ppermute x3, starting transfers between devices, body(): lax.ppermute(value, 'pt', swap)  6.25 us
    unnamed x13, local copies, waits for them, and re-layouts  2.22 us
  transfers between devices with their start and end apart: 7, of which 2 were waited for; matrix products, arithmetic and copies ran while one was open for 0% of the time, Pallas kernels for 0%

profile of v3, /device:TPU:6, one launch (start us, length us, event | category | flops | bytes accessed | tf_op | source)
XLA Modules:
  0.0 96.7 jit_solution(17823872151281222089)
XLA Ops:
  0.6 0.9 copy.11
  1.5 0.0 copy-start.2
  1.5 0.0 copy-start.1
  1.6 0.6 copy-done.2
  2.2 0.0 copy-done.1
  2.2 10.6 %collective-permute-start.2 = (f32[144,128]{1,0:T(8,128)S(1)}, f32[144,128]{1,0:T(8,128)S(1)}, u32[]{:S(2)}, u32[]{:S(2)}) collective-permute-start(f32[144,128]{1,0:T(8,128)S(1)} %pad_maximum_fusion.refs_3_), channel_id=1, source_target_pairs={{8,16},{16,8},{24,32},{32,24},{40,48},{48,40},{56,64},{64,56},{72,... | collective-permute-start | bytes 221192 | tf_op jit(solution)/shard_map/ppermute | solution.py:196
  12.9 1.9 %collective-permute-start.1 = (f32[144,128]{1,0:T(8,128)S(1)}, f32[144,128]{1,0:T(8,128)S(1)}, u32[]{:S(2)}, u32[]{:S(2)}) collective-permute-start(f32[144,128]{1,0:T(8,128)S(1)} %pad_maximum_fusion.refs_3_), channel_id=1, source_target_pairs={{0,16},{16,32},{24,8},{32,48},{40,24},{48,64},{56,40},{64,80},{72,... | collective-permute-start | bytes 221192 | tf_op jit(solution)/shard_map/ppermute | solution.py:196
  14.8 3.9 %collective-permute-start = (f32[144,128]{1,0:T(8,128)S(1)}, f32[144,128]{1,0:T(8,128)S(1)}, u32[]{:S(2)}, u32[]{:S(2)}) collective-permute-start(f32[144,128]{1,0:T(8,128)S(1)} %pad_maximum_fusion.refs_3_), channel_id=1, source_target_pairs={{8,32},{24,48},{32,8},{40,64},{48,24},{56,80},{64,40},{72,96},{80,... | collective-permute-start | bytes 221192 | tf_op jit(solution)/shard_map/ppermute | solution.py:196
  18.7 1.9 %collective-permute-start.3 = (f32[144,128]{1,0:T(8,128)S(1)}, f32[144,128]{1,0:T(8,128)S(1)}, u32[]{:S(2)}, u32[]{:S(2)}) collective-permute-start(f32[144,128]{1,0:T(8,128)S(1)} %pad_maximum_fusion.refs_3_), channel_id=1, source_target_pairs={{0,8},{8,0},{16,24},{24,16},{32,40},{40,32},{48,56},{56,48},{64,72... | collective-permute-start | bytes 221192 | tf_op jit(solution)/shard_map/ppermute | solution.py:197
  20.7 0.7 copy-done.3
  21.4 0.1 fusion.4.index_ref
  21.5 0.1 mul.50
  21.6 0.1 reshape.46.refs_8_
  21.7 2.4 %collective-permute-start.4 = (f32[144,128]{1,0:T(8,128)S(1)}, f32[144,128]{1,0:T(8,128)S(1)}, u32[]{:S(2)}, u32[]{:S(2)}) collective-permute-start(f32[144,128]{1,0:T(8,128)S(1)} %collective-permute-done.2.refs_2_), channel_id=1, source_target_pairs={{0,8},{8,0},{16,24},{24,16},{32,40},{40,32},{48,56},{56,48},{64,72... | collective-permute-start | bytes 221192 | tf_op jit(solution)/shard_map/ppermute | solution.py:197
  24.2 1.9 %collective-permute-start.5 = (f32[144,128]{1,0:T(8,128)S(1)}, f32[144,128]{1,0:T(8,128)S(1)}, u32[]{:S(2)}, u32[]{:S(2)}) collective-permute-start(f32[144,128]{1,0:T(8,128)S(1)} %collective-permute-done.1.refs_1_), channel_id=1, source_target_pairs={{0,8},{8,0},{16,24},{24,16},{32,40},{40,32},{48,56},{56,48},{64,72... | collective-permute-start | bytes 221192 | tf_op jit(solution)/shard_map/ppermute | solution.py:197
  26.1 0.1 pad_add_fusion.place_ref
  26.2 1.1 %collective-permute-done.5.refs_6_ = f32[144,128]{1,0:T(8,128)S(1)} collective-permute-done((f32[144,128]{1,0:T(8,128)S(1)}, f32[144,128]{1,0:T(8,128)S(1)}, u32[]{:S(2)}, u32[]{:S(2)}) %collective-permute-start.5) | collective-permute-done | bytes 73760 | tf_op jit(solution)/shard_map/ppermute | solution.py:197
  27.3 0.1 broadcast_in_dim.29.refs_9_
  27.4 19.7 %farm.1 = (f32[16,1024]{1,0:T(8,128)}, f32[8,128]{1,0:T(8,128)S(1)}, f32[8,2,8,128]{3,2,1,0:T(8,128)S(1)}) custom-call(s32[8,16]{1,0:T(8,128)S(1)} %fusion.4.index_ref, s32[8]{0:T(128)S(1)} %and_select_fusion.pairs_ref, s32[2]{0:T(128)S(1)} %pad_add_fusion.place_ref, f32[144,128]{1,0:T(8,128)S(1)} %collective-permute-done.refs_0_, ...), custom_call_target="tpu_custom_call" | custom-call | flops 1073741824 | bytes 4194304 | tf_op jit(solution)/shard_map/farm/pallas_call | solution.py:162
  47.1 8.3 %all_to_all.10 = f32[8,2,8,128]{3,2,1,0:T(8,128)S(1)} all-to-all(f32[8,2,8,128]{3,2,1,0:T(8,128)S(1)} %get-tuple-element.7), channel_id=1, replica_groups={{0,8,16,24,32,40,48,56},{64,72,80,88,96,104,112,120},{128,136,144,152,1..., dimensions={0} | all-to-all | bytes 131072 | tf_op jit(solution)/shard_map/all_to_all | solution.py:211
  55.4 19.0 %collective-permute-start.6 = (f32[8,128]{1,0:T(8,128)S(1)}, f32[8,128]{1,0:T(8,128)S(1)}, u32[]{:S(2)}, u32[]{:S(2)}) collective-permute-start(f32[8,128]{1,0:T(8,128)S(1)} %slice_bitcast_fusion), channel_id=1, source_target_pairs={{40,64},{64,40},{48,72},{72,48},{56,80},{80,56},{104,128},{128,104... | collective-permute-start | bytes 12296 | tf_op jit(solution)/shard_map/ppermute | solution.py:216
  74.4 1.3 %collective-permute-done.6 = f32[8,128]{1,0:T(8,128)S(1)} collective-permute-done((f32[8,128]{1,0:T(8,128)S(1)}, f32[8,128]{1,0:T(8,128)S(1)}, u32[]{:S(2)}, u32[]{:S(2)}) %collective-permute-start.6) | collective-permute-done | bytes 4128 | tf_op jit(solution)/shard_map/ppermute | solution.py:216
  75.7 20.4 %all_to_all.11 = f32[8,8,128]{2,1,0:T(8,128)S(1)} all-to-all(f32[8,8,128]{2,1,0:T(8,128)S(1)} %broadcast_in_dim.31), channel_id=1, replica_groups=mesh['pt'=64,'dir'=8] {'dir'}, dimensions={0} | all-to-all | bytes 65536 | tf_op jit(solution)/shard_map/all_to_all | solution.py:219
  96.1 0.6 reduce_sum.19
  (21 shorter events, 0.1 us)
Async XLA Ops:
  0.6 0.9 copy-start
  1.5 0.7 copy-start.2
  1.5 0.7 copy-start.1
  2.2 19.5 %collective-permute-start.2 = (f32[144,128]{1,0:T(8,128)S(1)}, f32[144,128]{1,0:T(8,128)S(1)}, u32[]{:S(2)}, u32[]{:S(2)}) collective-permute-start(f32[144,128]{1,0:T(8,128)S(1)} %pad_maximum_fusion.refs_3_), channel_id=1, source_target_pairs={{8,16},{16,8},{24,32},{32,24},{40,48},{48,40},{56,64},{64,56},{72,... | collective-permute-start | bytes 221192 | tf_op jit(solution)/shard_map/ppermute | solution.py:196
  12.9 11.3 %collective-permute-start.1 = (f32[144,128]{1,0:T(8,128)S(1)}, f32[144,128]{1,0:T(8,128)S(1)}, u32[]{:S(2)}, u32[]{:S(2)}) collective-permute-start(f32[144,128]{1,0:T(8,128)S(1)} %pad_maximum_fusion.refs_3_), channel_id=1, source_target_pairs={{0,16},{16,32},{24,8},{32,48},{40,24},{48,64},{56,40},{64,80},{72,... | collective-permute-start | bytes 221192 | tf_op jit(solution)/shard_map/ppermute | solution.py:196
  14.8 11.4 %collective-permute-start = (f32[144,128]{1,0:T(8,128)S(1)}, f32[144,128]{1,0:T(8,128)S(1)}, u32[]{:S(2)}, u32[]{:S(2)}) collective-permute-start(f32[144,128]{1,0:T(8,128)S(1)} %pad_maximum_fusion.refs_3_), channel_id=1, source_target_pairs={{8,32},{24,48},{32,8},{40,64},{48,24},{56,80},{64,40},{72,96},{80,... | collective-permute-start | bytes 221192 | tf_op jit(solution)/shard_map/ppermute | solution.py:196
  18.7 7.4 %collective-permute-start.3 = (f32[144,128]{1,0:T(8,128)S(1)}, f32[144,128]{1,0:T(8,128)S(1)}, u32[]{:S(2)}, u32[]{:S(2)}) collective-permute-start(f32[144,128]{1,0:T(8,128)S(1)} %pad_maximum_fusion.refs_3_), channel_id=1, source_target_pairs={{0,8},{8,0},{16,24},{24,16},{32,40},{40,32},{48,56},{56,48},{64,72... | collective-permute-start | bytes 221192 | tf_op jit(solution)/shard_map/ppermute | solution.py:197
  20.7 0.7 copy-start.3
  20.7 0.7 copy-start.4
  21.7 4.4 %collective-permute-start.4 = (f32[144,128]{1,0:T(8,128)S(1)}, f32[144,128]{1,0:T(8,128)S(1)}, u32[]{:S(2)}, u32[]{:S(2)}) collective-permute-start(f32[144,128]{1,0:T(8,128)S(1)} %collective-permute-done.2.refs_2_), channel_id=1, source_target_pairs={{0,8},{8,0},{16,24},{24,16},{32,40},{40,32},{48,56},{56,48},{64,72... | collective-permute-start | bytes 221192 | tf_op jit(solution)/shard_map/ppermute | solution.py:197
  24.2 3.2 %collective-permute-start.5 = (f32[144,128]{1,0:T(8,128)S(1)}, f32[144,128]{1,0:T(8,128)S(1)}, u32[]{:S(2)}, u32[]{:S(2)}) collective-permute-start(f32[144,128]{1,0:T(8,128)S(1)} %collective-permute-done.1.refs_1_), channel_id=1, source_target_pairs={{0,8},{8,0},{16,24},{24,16},{32,40},{40,32},{48,56},{56,48},{64,72... | collective-permute-start | bytes 221192 | tf_op jit(solution)/shard_map/ppermute | solution.py:197
  26.2 1.2 %copy-start.5 = (f32[1,16]{1,0:T(1,128)S(1)}, f32[1,16]{1,0:T(1,128)}, u32[]{:S(2)}) copy-start(f32[1,16]{1,0:T(1,128)} %param.11) | copy-start | bytes 196
  55.4 20.3 %collective-permute-start.6 = (f32[8,128]{1,0:T(8,128)S(1)}, f32[8,128]{1,0:T(8,128)S(1)}, u32[]{:S(2)}, u32[]{:S(2)}) collective-permute-start(f32[8,128]{1,0:T(8,128)S(1)} %slice_bitcast_fusion), channel_id=1, source_target_pairs={{40,64},{64,40},{48,72},{72,48},{56,80},{80,56},{104,128},{128,104... | collective-permute-start | bytes 12296 | tf_op jit(solution)/shard_map/ppermute | solution.py:216
